TPU v7x, 256 devices: a whole 4x4x8 slice. The times are simulated.
256 devices in a mesh: frames: 32 (over z, y), heads: 8 (over x, core).
Axes of the slice: x: 4, y: 4, z: 8, core: 2. Of those that a mesh axis runs over, the one named last changes fastest.
Arguments:
- bank_query: bfloat16 [64, 256, 5120], P(None, 'frames', 'heads'), may hold values from -2048 to 2048
- char_bank: bfloat16 [2, 8, 768, 5120], P(None, None, 'frames', 'heads'), may hold values from -8 to 8
- char_slots: int32 [32, 2], replicated, may hold values from 0 to 7, as said below
- slot_live: int32 [32, 2], replicated, may hold values from 0 to 1, as said below
- frame_tokens: bfloat16 [3, 64, 256, 5120], P(None, None, 'frames', 'heads'), may hold values from -2048 to 2048
- out_weight: bfloat16 [5120, 5120], P('heads'), may hold values from -0.078125 to 0.078125
Outputs:
- blended: bfloat16 [64, 256, 5120], P('heads', 'frames')
Inputs may be any that keep to these rules, and one draw needn't show every extreme that they name: `char_slots`: the two ids of a shard differ. `slot_live`: slot 0 of every shard is 1.
All inputs are finite; a program needn't handle non-finite values.
Results may differ from a plain program's by a relative error of at most 0.014.
Values may be sent and summed in bfloat16 or wider, within the bound.
A program may use at most 128 MiB of HBM per device.

v0:
```python
import jax
import jax.numpy as jnp
from jax import lax
from jax.sharding import PartitionSpec as P

HEAD_DIM = 128


def absorb(running, queries, key_rows, value_rows, slot_open):
    peak, totals, gathered = running
    scores = jnp.einsum(
        "qhd,khd->qhk", queries, key_rows, preferred_element_type=jnp.float32
    ) * HEAD_DIM ** (-0.5)
    new_peak = jnp.maximum(peak, jnp.max(scores, axis=-1))
    weights = jnp.exp(scores - new_peak[..., None])
    rescale = jnp.exp(peak - new_peak)
    new_totals = totals * rescale + jnp.sum(weights, axis=-1)
    new_gathered = gathered * rescale[..., None] + jnp.einsum(
        "qhk,khd->qhd", weights.astype(jnp.bfloat16), value_rows, preferred_element_type=jnp.float32
    )
    return (
        jnp.where(slot_open, new_peak, peak),
        jnp.where(slot_open, new_totals, totals),
        jnp.where(slot_open, new_gathered, gathered),
    )


def frame_attend(arrived):
    queries = arrived[0]
    key_rows = arrived[1]
    value_rows = arrived[2]
    scores = jnp.einsum(
        "sfhd,sghd->sfhg", queries, key_rows, preferred_element_type=jnp.float32
    ) * HEAD_DIM ** (-0.5)
    peak = jnp.max(scores, axis=-1, keepdims=True)
    weights = jnp.exp(scores - peak)
    totals = jnp.sum(weights, axis=-1, keepdims=True)
    attended = (
        jnp.einsum(
            "sfhg,sghd->sfhd",
            weights.astype(jnp.bfloat16),
            value_rows,
            preferred_element_type=jnp.float32,
        )
        / totals
    )
    attended = attended.astype(jnp.bfloat16)
    return lax.all_to_all(attended, "frames", split_axis=1, concat_axis=0, tiled=True)


def local(bank_query, char_bank, char_slots, slot_live, frame_tokens, out_weight):
    spatial, frames_here, local_width = bank_query.shape
    heads_here = local_width // HEAD_DIM
    row_total = spatial * frames_here
    queries = bank_query.reshape(row_total, heads_here, HEAD_DIM)
    shard_index = lax.axis_index("frames")
    opened = lax.dynamic_index_in_dim(slot_live, shard_index, 0, keepdims=False) > 0
    start_state = (
        jnp.full((row_total, heads_here), -1e30, jnp.float32),
        jnp.zeros((row_total, heads_here), jnp.float32),
        jnp.zeros((row_total, heads_here, HEAD_DIM), jnp.float32),
    )
    outgoing = jnp.take(char_bank, char_slots.T, axis=1)
    arrived = lax.all_to_all(outgoing, "frames", split_axis=2, concat_axis=3, tiled=True)
    running = start_state
    for slot_index in range(2):
        key_rows = arrived[0, slot_index, 0].reshape(-1, heads_here, HEAD_DIM)
        value_rows = arrived[1, slot_index, 0].reshape(-1, heads_here, HEAD_DIM)
        running = absorb(running, queries, key_rows, value_rows, opened[slot_index])
    peak, totals, gathered = running
    ref_out = gathered / totals[..., None]
    token_block = frame_tokens.reshape(3, spatial, frames_here, heads_here, HEAD_DIM)
    frame_out = frame_attend(
        lax.all_to_all(token_block, "frames", split_axis=1, concat_axis=2, tiled=True)
    )
    combined = (
        ref_out + frame_out.reshape(row_total, heads_here, HEAD_DIM).astype(jnp.float32)
    ).astype(jnp.bfloat16)
    combined = combined.reshape(row_total, local_width)
    head_count = lax.axis_size("heads")
    summed = lax.psum_scatter(
        jnp.dot(combined, out_weight, preferred_element_type=jnp.float32).astype(jnp.bfloat16),
        "heads",
        scatter_dimension=0,
        tiled=True,
    ).astype(jnp.float32)
    return summed.reshape(spatial // head_count, frames_here, -1).astype(jnp.bfloat16)


def solution(mesh):
    in_specs = (
        P(None, "frames", "heads"),
        P(None, None, "frames", "heads"),
        P(),
        P(),
        P(None, None, "frames", "heads"),
        P("heads", None),
    )
    out_specs = P("heads", "frames", None)
    return jax.shard_map(local, mesh=mesh, in_specs=in_specs, out_specs=out_specs, check_vma=False)
```

profile of v0, /device:TPU:8, one launch (start us, length us, event | category | flops | bytes accessed | tf_op | source)
XLA Modules:
  0.0 284.1 jit_solution(11550030958785814615)
XLA Ops:
  6.5 0.0 copy-start
  6.5 1.9 copy.84
  8.5 59.2 %all_to_all.36 = bf16[3,64,8,5,128]{4,2,3,0,1:T(8,128)(2,1)S(1)} all-to-all(bf16[3,64,8,5,128]{4,2,3,0,1:T(8,128)(2,1)S(1)} %copy.84), channel_id=1, replica_groups=mesh['frames'=32,'heads'=8] {'frames'}, dimensions={1} | all-to-all | bytes 3932160 | tf_op jit(solution)/shard_map/all_to_all | solution.py:74
  67.7 0.3 copy.85
  68.0 0.3 fusion.54
  68.4 0.5 bitcast_reduce_fusion.2
  68.9 0.4 fusion.15
  69.4 0.0 copy-start.5
  69.4 0.9 fusion.30
  70.3 1.5 copy.90
  71.8 5.6 %all-to-all-start.2 = ((bf16[2,256,5,128]{3,0,2,1:T(2,128)(2,1)}), bf16[2,256,5,128]{3,0,2,1:T(2,128)(2,1)S(1)}, u32[]{:S(2)}, u32[]{:S(2)}) async-start(bf16[2,256,5,128]{3,0,2,1:T(2,128)(2,1)} %copy.90), calls=%async_computation.2 | async-start | bytes 1310720 | tf_op jit(solution)/shard_map/all_to_all | solution.py:48
  77.4 0.0 copy-done.5
  77.4 0.1 reshape.79
  77.5 0.0 copy-done
  77.5 2.9 %gather_fusion = bf16[64,2,24,640]{3,2,1,0:T(8,128)(2,1)} fusion(bf16[2,8,24,640]{3,2,1,0:T(8,128)(2,1)S(1)} %copy-done, s32[1024]{0:T(1024)S(1)} %pad_clamp_fusion), kind=kCustom, calls=%fused_computation | custom fusion | bytes 7864576 | tf_op jit(solution)/shard_map/jit(_take)/gather | solution.py:63
  80.4 2.6 select_bitcast_fusion
  83.0 2.2 copy.72
  85.3 10.8 %all-to-all-done.2 = bf16[2,256,5,128]{3,0,2,1:T(2,128)(2,1)S(1)} async-done(((bf16[2,256,5,128]{3,0,2,1:T(2,128)(2,1)}), bf16[2,256,5,128]{3,0,2,1:T(2,128)(2,1)S(1)}, u32[]{:S(2)}, u32[]{:S(2)}) %all-to-all-start.2) | async-done | bytes 655392 | tf_op jit(solution)/shard_map/all_to_all | solution.py:48
  96.1 5.6 %all-to-all-start = ((bf16[2,2,32,24,640]{4,3,1,0,2:T(8,128)(2,1)}), bf16[2,2,32,24,640]{4,3,1,0,2:T(8,128)(2,1)}, u32[]{:S(2)}, u32[]{:S(2)}) async-start(bf16[2,2,32,24,640]{4,3,1,0,2:T(8,128)(2,1)} %copy.72), calls=%async_computation | async-start | bytes 7864320 | tf_op jit(solution)/shard_map/all_to_all | solution.py:64
  101.7 0.2 reduce-scatter.2.cloned.1.call-start
  102.0 0.7 reshape.72
  102.7 0.0 copy-done.6
  102.7 0.1 dynamic-slice_compare_fusion
  102.8 0.5 fusion.55
  103.3 0.1 convert_bitcast_fusion
  103.4 0.1 copy.92
  103.5 1.5 copy.93
  105.0 83.2 %all-to-all-done = bf16[2,2,32,24,640]{4,3,1,0,2:T(8,128)(2,1)} async-done(((bf16[2,2,32,24,640]{4,3,1,0,2:T(8,128)(2,1)}), bf16[2,2,32,24,640]{4,3,1,0,2:T(8,128)(2,1)}, u32[]{:S(2)}, u32[]{:S(2)}) %all-to-all-start) | async-done | bytes 3932192 | tf_op jit(solution)/shard_map/all_to_all | solution.py:64
  188.2 2.5 copy.73
  190.7 1.7 fusion.53
  192.4 2.4 copy.79
  194.7 2.3 copy.74
  197.0 5.6 %bitcast_reduce_fusion = (f32[512,5]{0,1:T(8,128)S(1)}, f32[5,768,512]{2,1,0:T(8,128)}) fusion(bf16[768,5,128]{0,2,1:T(8,128)(2,1)} %bitcast.111, bf16[512,5,128]{2,1,0:T(8,128)(2,1)S(1)} %reshape.72), kind=kOutput, calls=%fused_computation.2 | convolution fusion | flops 507246080 | bytes 9512960 | tf_op jit(solution)/shard_map/qhd,khd->qhk/dot_general | solution.py:11
  202.6 0.0 copy-done.2
  202.6 4.4 %bitcast_reduce_fusion.1 = (f32[512,5]{0,1:T(8,128)S(1)}, f32[5,768,512]{2,1,0:T(8,128)}) fusion(bf16[768,5,128]{0,2,1:T(8,128)(2,1)S(1)} %bitcast.110, bf16[512,5,128]{2,1,0:T(8,128)(2,1)S(1)} %reshape.72), kind=kOutput, calls=%fused_computation.5 | convolution fusion | flops 507246080 | bytes 9512960 | tf_op jit(solution)/shard_map/qhd,khd->qhk/dot_general | solution.py:11
  207.0 0.6 copy.77
  207.7 0.6 copy.82
  208.3 0.6 select_maximum_fusion
  208.9 6.9 %fusion.2 = (f32[512,5]{0,1:T(8,128)S(1)}, f32[512,5]{0,1:T(8,128)S(1)}) fusion(f32[5,768,512]{2,1,0:T(8,128)} %get-tuple-element.24, f32[512,5]{0,1:T(8,128)S(1)} %get-tuple-element.16, f32[512,5]{0,1:T(8,128)S(1)} %get-tuple-element.15, f32[5,768,512]{2,1,0:T(8,128)} %get-tuple-element.22), kind=kLoop, calls=%fused_computation.8 | loop fusion | flops 11791360 | bytes 15769600 | tf_op jit(solution)/shard_map/reduce_sum | solution.py:17
  215.8 1.3 add_select_fusion
  217.1 0.0 slice-start
  217.1 6.0 %fusion.34 = f32[512,5,128]{0,2,1:T(8,128)S(1)} fusion(bf16[768,5,128]{0,2,1:T(8,128)(2,1)S(1)} %bitcast.109, f32[5,768,512]{2,1,0:T(8,128)} %get-tuple-element.24, f32[512,5]{0,1:T(8,128)S(1)} %get-tuple-element.16, f32[512,5]{0,1:T(8,128)S(1)} %get-tuple-element.14, pred[]{:T(512)} %bitcast.1), kind=kOutput, calls=%fused_computation.35 | convolution fusion | flops 509870080 | bytes 10178561 | tf_op jit(solution)/shard_map/qhk,khd->qhd/dot_general | solution.py:18
  223.2 0.0 slice-start.1
  223.2 5.8 %add_convert_fusion = bf16[512,5,128]{0,2,1:T(8,128)(2,1)S(1)} fusion(f32[512,5,128]{0,2,1:T(8,128)S(1)} %copy-done.3, f32[512,5,128]{0,2,1:T(8,128)S(1)} %fusion.34, bf16[768,5,128]{0,2,1:T(8,128)(2,1)S(1)} %bitcast.113, f32[5,768,512]{2,1,0:T(8,128)} %get-tuple-element.22, f32[512,5]{0,1:T(8,128)S(1)} %get-tuple-element.15, ...), kind=kOutput, calls=%fused_computation.32 | convolution fusion | flops 511180800 | bytes 12154881 | tf_op jit(solution)/shard_map/qhk,khd->qhd/dot_general | solution.py:18
  229.0 0.0 copy-start.1
  229.0 6.1 %convolution_convert_fusion = bf16[512,5120]{1,0:T(8,128)(2,1)} fusion(bf16[512,640]{0,1:T(8,128)(2,1)S(1)} %bitcast.116, bf16[640,5120]{1,0:T(8,128)(2,1)S(1)} %bitcast.115), kind=kOutput, calls=%fused_computation.7 | convolution fusion | flops 3358064640 | bytes 12451840 | tf_op jit(solution)/shard_map/dot_general | solution.py:82
  235.1 0.0 reduce-scatter.2.cloned.1.call-update
  235.1 42.1 %reduce-scatter.2.cloned.1.call-done = bf16[64,5120]{1,0:T(8,128)(2,1)} async-done(((bf16[512,5120]{1,0:T(8,128)(2,1)}), bf16[64,5120]{1,0:T(8,128)(2,1)}) %reduce-scatter.2.cloned.1.call-update) | async-done | bytes 655376 | tf_op jit(solution)/shard_map/reduce_scatter | solution.py:81
  (13 shorter events, 0.0 us)
Async XLA Ops:
  6.5 71.0 %copy-start = (bf16[2,8,24,640]{3,2,1,0:T(8,128)(2,1)S(1)}, bf16[2,8,24,640]{3,2,1,0:T(8,128)(2,1)}, u32[]{:S(2)}) copy-start(bf16[2,8,24,640]{3,2,1,0:T(8,128)(2,1)} %param.7) | copy-start | bytes 1474564
  69.4 8.0 %copy-start.5 = (s32[32,2]{0,1:T(2,128)S(1)}, s32[32,2]{0,1:T(2,128)}, u32[]{:S(2)}) copy-start(s32[32,2]{0,1:T(2,128)} %param.8) | copy-start | bytes 772
  71.8 24.3 %all-to-all-start.2 = ((bf16[2,256,5,128]{3,0,2,1:T(2,128)(2,1)}), bf16[2,256,5,128]{3,0,2,1:T(2,128)(2,1)S(1)}, u32[]{:S(2)}, u32[]{:S(2)}) async-start(bf16[2,256,5,128]{3,0,2,1:T(2,128)(2,1)} %copy.90), calls=%async_computation.2 | async-start | bytes 1310720 | tf_op jit(solution)/shard_map/all_to_all | solution.py:48
  85.3 16.7 %copy-start.4 = (bf16[64,8,640]{2,1,0:T(8,128)(2,1)S(1)}, bf16[64,8,640]{2,1,0:T(8,128)(2,1)}, u32[]{:S(2)}) copy-start(bf16[64,8,640]{2,1,0:T(8,128)(2,1)} %param.6) | copy-start | bytes 1966084
  85.3 17.4 %copy-start.6 = (s32[32,2]{0,1:T(2,128)S(1)}, s32[32,2]{0,1:T(2,128)}, u32[]{:S(2)}) copy-start(s32[32,2]{0,1:T(2,128)} %param.9) | copy-start | bytes 772
  96.1 92.1 %all-to-all-start = ((bf16[2,2,32,24,640]{4,3,1,0,2:T(8,128)(2,1)}), bf16[2,2,32,24,640]{4,3,1,0,2:T(8,128)(2,1)}, u32[]{:S(2)}, u32[]{:S(2)}) async-start(bf16[2,2,32,24,640]{4,3,1,0,2:T(8,128)(2,1)} %copy.72), calls=%async_computation | async-start | bytes 7864320 | tf_op jit(solution)/shard_map/all_to_all | solution.py:64
  101.7 175.6 %reduce-scatter.2.cloned.1.call-start = ((), (), s32[]{:S(2)}) async-start(), calls=%async_computation.4 | async-start | bytes 5898240 | tf_op jit(solution)/shard_map/reduce_scatter | solution.py:81
  197.0 5.6 %copy-start.2 = (bf16[1,1,1,768,640]{3,4,2,1,0:T(8,128)(2,1)S(1)}, bf16[1,1,1,768,640]{3,4,2,1,0:T(8,128)(2,1)}, u32[]{:S(2)}) copy-start(bf16[1,1,1,768,640]{3,4,2,1,0:T(8,128)(2,1)} %copy.74) | copy-start | bytes 2949124
  217.1 6.0 %copy-start.3 = (f32[512,5,128]{0,2,1:T(8,128)S(1)}, f32[512,5,128]{0,2,1:T(8,128)}, u32[]{:S(2)}) copy-start(f32[512,5,128]{0,2,1:T(8,128)} %copy.93) | copy-start | bytes 3932164
  217.1 11.8 %slice-start = ((s8[6553600]{0:T(1024)(128)(4,1)}), s8[4194304]{0:T(1024)(128)(4,1)S(1)}, s32[]{:S(2)}) async-start(s8[6553600]{0:T(1024)(128)(4,1)} %bitcast.114), calls=%async_computation.5 | async-start | bytes 8388608
  223.2 5.8 %slice-start.1 = ((s8[6553600]{0:T(1024)(128)(4,1)}), s8[2359296]{0:T(1024)(128)(4,1)S(1)}, s32[]{:S(2)}) async-start(s8[6553600]{0:T(1024)(128)(4,1)} %bitcast.114), calls=%async_computation.6 | async-start | bytes 4718592
  229.0 48.3 %copy-start.1 = (bf16[2,8,24,640]{3,2,1,0:T(8,128)(2,1)S(1)}, bf16[2,8,24,640]{3,2,1,0:T(8,128)(2,1)}, u32[]{:S(2)}) copy-start(bf16[2,8,24,640]{3,2,1,0:T(8,128)(2,1)} %param.7) | copy-start | bytes 1474564
Sparse Core Ops, SparseCore 0:
  235.3 41.9 reduce-scatter.1
where the time goes:
time: 285 us; the launch traced here: 284 us
  waiting for transfers between devices  136 us (48%)
  blocking collectives  59.2 us (21%)
  matrix products  29.3 us (10%)
  local copies, waits for them, and re-layouts  22.3 us (8%)
  between operations  13.7 us (5%)
  other arithmetic  12 us (4%)
  starting transfers between devices  11.4 us (4%)
    all_to_all x1, waiting for transfers between devices, local(): lax.all_to_all(outgoing, 'frames', split_axis=2, concat_axis=3, tiled=True)  83.2 us
    all_to_all x1, blocking collectives, local(): lax.all_to_all(token_block, 'frames', split_axis=1, concat_axis=2, tiled=...  59.2 us
    reduce_scatter x1, waiting for transfers between devices, local(): lax.psum_scatter(jnp.dot(combined, out_weight, preferred_element_type=jnp...  42.1 us
    dot_general x2, matrix products, absorb(): jnp.einsum('qhk,khd->qhd', weights.astype(jnp.bfloat16), value_rows, pref...  11.8 us
    all_to_all x1, waiting for transfers between devices, frame_attend(): lax.all_to_all(attended, 'frames', split_axis=1, concat_axis=0, tiled=True)  10.8 us
    dot_general x2, matrix products, absorb(): jnp.einsum('qhd,khd->qhk', queries, key_rows, preferred_element_type=jnp....  9.97 us
    reduce_sum x1, other arithmetic, absorb(): new_totals = totals * rescale + jnp.sum(weights, axis=-1)  6.86 us
    slice x3, local copies, waits for them, and re-layouts, local(): key_rows = arrived[0, slot_index, 0].reshape(-1, heads_here, HEAD_DIM)  6.36 us
  transfers between devices with their start and end apart: 3, of which 3 were waited for; matrix products, arithmetic and copies ran while one was open for 4% of the time, Pallas kernels for 0%

commit v1 on v0

v1 whole, which is shorter than its diff:
```python
import functools

import jax
import jax.numpy as jnp
from jax import lax
from jax.experimental import pallas as pl
from jax.experimental.pallas import tpu as pltpu
from jax.sharding import PartitionSpec as P

HEAD_DIM = 128
ROWS_Y = 4
EXP2_SCALE = HEAD_DIM ** -0.5 * 1.4426950408889634
FAR = 1e30
MESH = pl.DeviceIdType.MESH


def dot_t(a, b):
    return lax.dot_general(a, b, (((1,), (1,)), ((), ())), preferred_element_type=jnp.float32)


def dot(a, b):
    return jnp.dot(a, b, preferred_element_type=jnp.float32)


def await_bytes(ref, sem):
    pltpu.make_async_copy(ref, ref, sem).wait()


def kernel(dims, slots, live, queries, bank, tokens, weight, out, *scratch):
    shards, levels, chips = dims
    held = (scratch[0:levels], scratch[levels:2 * levels])
    (picked, listed, qv, wv, qkv, o_here, o_back, ref_out, combined, part, pair, summed, from_left_half,
     from_right_half, from_left, from_right, local_sem, ring_send, ring_recv, pick_send, pick_recv, token_send,
     token_recv, o_send, o_recv, pair_send, pair_recv, sum_send, sum_recv, own_sem) = scratch[2 * levels:]
    spatial, here, width = queries.shape
    heads = width // HEAD_DIM
    mine = spatial // shards
    f = lax.axis_index("frames")
    r = lax.axis_index("heads")
    z, y = lax.div(f, ROWS_Y), lax.rem(f, ROWS_Y)
    x, core = lax.div(r, 2), lax.rem(r, 2)
    up = lax.rem(z + 1, levels) * ROWS_Y + y
    down = lax.rem(z + levels - 1, levels) * ROWS_Y + y
    twin = r + 1 - 2 * core
    right = lax.rem(x + 1, chips) * 2 + core
    left = lax.rem(x + chips - 1, chips) * 2 + core

    def peer(i):
        k, dy = lax.div(i, ROWS_Y), lax.rem(i, ROWS_Y)
        odd = lax.rem(k, 2)
        dz = odd * lax.div(k + 1, 2) + (1 - odd) * (levels - lax.div(k, 2))
        return lax.rem(z + dz, levels) * ROWS_Y + lax.rem(y + dy, ROWS_Y)

    def remote(src, dst, send, recv, **where):
        copy = pltpu.make_async_remote_copy(
            src_ref=src, dst_ref=dst, send_sem=send, recv_sem=recv, device_id=where, device_id_type=MESH
        )
        copy.start()
        return copy

    own = [pltpu.make_async_copy(bank.at[kv], held[kv][0], local_sem.at[kv]) for kv in range(2)]
    load_q = pltpu.make_async_copy(queries, qv, local_sem.at[2])
    load_w = pltpu.make_async_copy(weight, wv, local_sem.at[3])
    keep = pltpu.make_async_copy(tokens.at[:, pl.ds(mine * f, mine)], qkv.at[:, :, f], local_sem.at[4])
    for copy in (*own, load_q, keep, load_w):
        copy.start()

    barrier = pltpu.get_barrier_semaphore()

    @pl.loop(1, shards)
    def _(i):
        pl.semaphore_signal(barrier, inc=1, device_id={"frames": peer(i)}, device_id_type=MESH)

    for near in (twin, right, left):
        pl.semaphore_signal(barrier, inc=1, device_id={"heads": near}, device_id_type=MESH)
    pl.semaphore_wait(barrier, shards - 1 + 3)

    half = levels // 2
    sends = []

    def pass_on(kv, src, rel, upward):
        ref = bank.at[kv] if src == 0 else held[kv][src]
        sends.append(
            remote(ref, held[kv][rel], ring_send.at[kv, rel], ring_recv.at[kv, rel], frames=up if upward else down)
        )

    def pick(kv, rel):
        for dy in range(ROWS_Y):
            shard = z * ROWS_Y + lax.rem(y + dy, ROWS_Y)
            for j in range(2):
                block = held[kv][rel][slots[shard, j]]
                if dy:
                    picked[kv, rel, dy - 1, j] = block
                else:
                    listed[kv, j, rel, 0] = block
        for dy in range(1, ROWS_Y):
            remote(
                picked.at[kv, rel, dy - 1], listed.at[kv, :, rel, dy], pick_send, pick_recv.at[kv],
                frames=z * ROWS_Y + lax.rem(y + dy, ROWS_Y),
            )

    for kv in range(2):
        pass_on(kv, 0, 1, True)
        pass_on(kv, 0, levels - 1, False)
    for kv in range(2):
        own[kv].wait()
        pick(kv, 0)

    def send_tokens():
        @pl.loop(1, shards)
        def _(i):
            p = peer(i)
            remote(tokens.at[:, pl.ds(mine * p, mine)], qkv.at[:, :, f], token_send, token_recv, frames=p)

    for step in range(1, half + 1):
        for kv in range(2):
            for rel, upward in ((step, True), (levels - step, False)):
                if step == half and upward != (kv == 0):
                    continue
                await_bytes(held[kv][rel], ring_recv.at[kv, rel])
                last = half if upward == (kv == 0) else half - 1
                if step < last:
                    pass_on(kv, rel, rel + 1 if upward else rel - 1, upward)
                if step < half:
                    pick(kv, rel)
        if step == half - 1:
            send_tokens()
    for kv in range(2):
        pick(kv, half)

    load_q.wait()
    for kv in range(2):
        await_bytes(listed.at[kv, :, :, pl.ds(1, ROWS_Y - 1)], pick_recv.at[kv])

    alive = live[f, 1] > 0
    keys = levels * ROWS_Y * listed.shape[4]

    def bank_head(h, _):
        hs = pl.ds(pl.multiple_of(h * HEAD_DIM, HEAD_DIM), HEAD_DIM)
        for block in range(2):
            rows = spatial // 2
            q = qv[pl.ds(block * rows, rows), :, hs].reshape(rows * here, HEAD_DIM)
            s0 = dot_t(q, listed[0, 0, :, :, :, hs].reshape(keys, HEAD_DIM))
            s1 = dot_t(q, listed[0, 1, :, :, :, hs].reshape(keys, HEAD_DIM))
            peak1 = jnp.max(s1, axis=1, keepdims=True)
            peak = jnp.max(s0, axis=1, keepdims=True)
            peak = jnp.where(alive, jnp.maximum(peak, peak1), peak)
            p0 = jnp.exp2((s0 - peak) * EXP2_SCALE)
            p1 = jnp.exp2((s1 - jnp.where(alive, peak, FAR)) * EXP2_SCALE)
            total = jnp.sum(p0, axis=1, keepdims=True) + jnp.sum(p1, axis=1, keepdims=True)
            got = dot(p0.astype(jnp.bfloat16), listed[1, 0, :, :, :, hs].reshape(keys, HEAD_DIM))
            got += dot(p1.astype(jnp.bfloat16), listed[1, 1, :, :, :, hs].reshape(keys, HEAD_DIM))
            ref_out[pl.ds(block * rows * here, rows * here), hs] = got / total
        return 0

    lax.fori_loop(0, heads, bank_head, 0)

    keep.wait()
    await_bytes(qkv.at[:, :, pl.ds(1, shards - 1)], token_recv)

    def frame_head(h, _):
        hs = pl.ds(pl.multiple_of(h * HEAD_DIM, HEAD_DIM), HEAD_DIM)
        for s in range(mine):
            q, k, v = (qkv[i, s, :, :, hs].reshape(shards * here, HEAD_DIM) for i in range(3))
            scores = dot_t(q, k)
            peak = jnp.max(scores, axis=1, keepdims=True)
            p = jnp.exp2((scores - peak) * EXP2_SCALE)
            got = dot(p.astype(jnp.bfloat16), v) / jnp.sum(p, axis=1, keepdims=True)
            o_here[s, :, :, hs] = got.astype(jnp.bfloat16).reshape(shards, here, HEAD_DIM)
        return 0

    lax.fori_loop(0, heads, frame_head, 0)

    @pl.loop(1, shards)
    def _(i):
        p = peer(i)
        remote(o_here.at[:, p], o_back.at[pl.ds(mine * f, mine)], o_send, o_recv, frames=p)

    keep_o = pltpu.make_async_copy(o_here.at[:, f], o_back.at[pl.ds(mine * f, mine)], own_sem)
    keep_o.start()
    keep_o.wait()
    load_w.wait()
    await_bytes(o_back.at[pl.ds(0, mine * (shards - 1))], o_recv)

    group = spatial * here // chips
    rows = group // 2
    order = (lax.rem(x + 2, chips), lax.rem(x + 1, chips), lax.rem(x + chips - 1, chips), x)
    columns = weight.shape[1]
    tile = 640
    pairs = []
    for k, dest in enumerate(order):
        at = pl.multiple_of(dest * group, group)
        combined[...] = (
            ref_out[pl.ds(at, group), :]
            + o_back[pl.ds(pl.multiple_of(dest * (spatial // chips), spatial // chips), spatial // chips)]
            .reshape(group, width).astype(jnp.float32)
        ).astype(jnp.bfloat16)

        @pl.loop(0, columns // tile)
        def _(n):
            cs = pl.ds(pl.multiple_of(n * tile, tile), tile)
            part[k, :, :, cs] = dot(combined[...], wv[:, cs]).astype(jnp.bfloat16).reshape(2, rows, tile)

        pairs.append(remote(part.at[k, 1 - core], pair.at[k], pair_send.at[k], pair_recv.at[k], heads=twin))

    def total(k, n, *more):
        cs = pl.ds(pl.multiple_of(n * tile, tile), tile)
        value = part[k, core, :, cs].astype(jnp.float32) + pair[k, :, cs].astype(jnp.float32)
        return value, cs

    h2 = rows // 2
    pairs[0].wait_recv()

    @pl.loop(0, columns // tile)
    def _(n):
        value, cs = total(0, n)
        summed[0, :, cs] = value.astype(jnp.bfloat16)

    sums = [
        remote(summed.at[0, pl.ds(0, h2)], from_left_half, sum_send.at[0], sum_recv.at[0], heads=right),
        remote(summed.at[0, pl.ds(h2, h2)], from_right_half, sum_send.at[1], sum_recv.at[1], heads=left),
    ]
    for k in (1, 2):
        pairs[k].wait_recv()
        await_bytes((from_left_half, from_right_half)[k - 1], sum_recv.at[k - 1])

        @pl.loop(0, columns // tile)
        def _(n):
            value, cs = total(k, n)
            top, bottom = value[:h2], value[h2:]
            if k == 1:
                top += from_left_half[:, cs].astype(jnp.float32)
            else:
                bottom += from_right_half[:, cs].astype(jnp.float32)
            summed[k, pl.ds(0, h2), cs] = top.astype(jnp.bfloat16)
            summed[k, pl.ds(h2, h2), cs] = bottom.astype(jnp.bfloat16)

        sums.append(
            remote(summed.at[k], (from_left, from_right)[k - 1], sum_send.at[k + 1], sum_recv.at[k + 1],
                   heads=(right, left)[k - 1])
        )
    pairs[3].wait_recv()
    await_bytes(from_left, sum_recv.at[2])
    await_bytes(from_right, sum_recv.at[3])

    @pl.loop(0, columns // tile)
    def _(n):
        value, cs = total(3, n)
        value += from_left[:, cs].astype(jnp.float32)
        value += from_right[:, cs].astype(jnp.float32)
        out[:, cs] = value.astype(jnp.bfloat16)

    for copy in (*sends, *pairs, *sums):
        copy.wait_send()
    await_bytes(picked, pick_send)
    await_bytes(tokens.at[:, pl.ds(0, mine * (shards - 1))], token_send)
    await_bytes(o_back.at[pl.ds(0, mine * (shards - 1))], o_send)


def local(dims, bank_query, char_bank, char_slots, slot_live, frame_tokens, out_weight):
    shards, levels, chips = dims
    spatial, here, width = bank_query.shape
    _, characters, ref_here, _ = char_bank.shape
    mine = spatial // shards
    columns = out_weight.shape[1]
    group = spatial * here // chips
    rows = group // 2
    bf16, f32 = jnp.bfloat16, jnp.float32
    dma = pltpu.SemaphoreType.DMA
    scratch = [pltpu.VMEM((characters, ref_here, width), bf16) for _ in range(2 * levels)] + [
        pltpu.VMEM((2, levels, ROWS_Y - 1, 2, ref_here, width), bf16),
        pltpu.VMEM((2, 2, levels, ROWS_Y, ref_here, width), bf16),
        pltpu.VMEM((spatial, here, width), bf16),
        pltpu.VMEM((width, columns), bf16),
        pltpu.VMEM((3, mine, shards, here, width), bf16),
        pltpu.VMEM((mine, shards, here, width), bf16),
        pltpu.VMEM((spatial, here, width), bf16),
        pltpu.VMEM((spatial * here, width), f32),
        pltpu.VMEM((group, width), bf16),
        pltpu.VMEM((chips, 2, rows, columns), bf16),
        pltpu.VMEM((chips, rows, columns), bf16),
        pltpu.VMEM((3, rows, columns), bf16),
        pltpu.VMEM((rows // 2, columns), bf16),
        pltpu.VMEM((rows // 2, columns), bf16),
        pltpu.VMEM((rows, columns), bf16),
        pltpu.VMEM((rows, columns), bf16),
        dma((5,)), dma((2, levels)), dma((2, levels)), dma(()), dma((2,)), dma(()), dma(()), dma(()), dma(()),
        dma((chips,)), dma((chips,)), dma((4,)), dma((4,)), dma(()),
    ]
    smem = pl.BlockSpec(memory_space=pltpu.SMEM)
    anywhere = pl.BlockSpec(memory_space=pl.ANY)
    out = pl.pallas_call(
        functools.partial(kernel, dims),
        out_shape=jax.ShapeDtypeStruct((rows, columns), bf16),
        in_specs=[smem, smem, anywhere, anywhere, anywhere, anywhere],
        out_specs=pl.BlockSpec(memory_space=pltpu.VMEM),
        scratch_shapes=scratch,
        compiler_params=pltpu.CompilerParams(
            collective_id=0, has_side_effects=True, vmem_limit_bytes=60 * 1024 * 1024
        ),
        name="block",
    )(char_slots, slot_live, bank_query, char_bank, frame_tokens, out_weight)
    return out.reshape(rows // here, here, columns)


def solution(mesh):
    shards = mesh.shape["frames"]
    dims = (shards, shards // ROWS_Y, mesh.shape["heads"] // 2)
    in_specs = (
        P(None, "frames", "heads"),
        P(None, None, "frames", "heads"),
        P(),
        P(),
        P(None, None, "frames", "heads"),
        P("heads", None),
    )
    return jax.shard_map(
        functools.partial(local, dims), mesh=mesh, in_specs=in_specs, out_specs=P("heads", "frames", None), check_vma=False
    )
```

time: 285 us -> 154 us (0.54)
  Pallas kernels: 0 us -> 146 us
  waiting for transfers between devices: 136 us -> 0 us
  blocking collectives: 59.2 us -> 0 us
  matrix products: 29.3 us -> 0 us
  local copies, waits for them, and re-layouts: 22.3 us -> 4.69 us
  between operations: 13.7 us -> 0.01 us
  other arithmetic: 12 us -> 0 us
  starting transfers between devices: 11.4 us -> 0 us
    pallas_call x0 -> x1, Pallas kernels: none -> 146 us  [local(): pl.pallas_call(functools.partial(kernel, dims), out_shape=jax.ShapeDtypeS...]
    all_to_all x2 -> x0, waiting for transfers between devices: 94 us -> none  [the longest x1 83.2 us: local(): lax.all_to_all(outgoing, 'frames', split_axis=2, concat_axis=3, tiled=True)]
    all_to_all x1 -> x0, blocking collectives: 59.2 us -> none  [local(): lax.all_to_all(token_block, 'frames', split_axis=1, concat_axis=2, tiled=...]
    reduce_scatter x1 -> x0, waiting for transfers between devices: 42.1 us -> none  [local(): lax.psum_scatter(jnp.dot(combined, out_weight, preferred_element_type=jnp...]
    dot_general x7 -> x0, matrix products: 29.3 us -> none  [the longest x2 11.8 us: absorb(): jnp.einsum('qhk,khd->qhd', weights.astype(jnp.bfloat16), value_rows, pref...]
    all_to_all x2 -> x0, starting transfers between devices: 11.2 us -> none  [the longest x1 5.62 us: local(): lax.all_to_all(outgoing, 'frames', split_axis=2, concat_axis=3, tiled=True)]
    slice x7 -> x0, local copies, waits for them, and re-layouts: 8.51 us -> none  [the longest x3 6.36 us: local(): key_rows = arrived[0, slot_index, 0].reshape(-1, heads_here, HEAD_DIM)]
    reduce_sum x2 -> x0, other arithmetic: 7.31 us -> none  [the longest x1 6.86 us: absorb(): new_totals = totals * rescale + jnp.sum(weights, axis=-1)]
  transfers between devices with their start and end apart: 3 -> 0, of which waited for: 3 -> 0; matrix products, arithmetic and copies ran while one was open for 4% -> 0% of each run, Pallas kernels for 0% -> 0%
where the time goes in v1:
time: 154 us; the launch traced here: 151 us
  Pallas kernels  146 us (95%)
  local copies, waits for them, and re-layouts  4.69 us (3%)
    pallas_call x1, Pallas kernels, local(): pl.pallas_call(functools.partial(kernel, dims), out_shape=jax.ShapeDtypeS...  146 us
    unnamed x3, local copies, waits for them, and re-layouts  4.69 us

profile of v1, /device:TPU:8, one launch (start us, length us, event | category | flops | bytes accessed | tf_op | source)
XLA Modules:
  0.0 150.7 jit_solution(8556391085086674817)
XLA Ops:
  0.0 1.4 copy.7.slots
  1.4 1.4 copy.8.live
  2.7 146.0 %block.1 = bf16[64,5120]{1,0:T(8,128)(2,1)} custom-call(s32[32,2]{1,0:T(8,128)} %copy.7.slots, s32[32,2]{1,0:T(8,128)} %copy.8.live, bf16[64,8,640]{2,1,0:T(8,128)(2,1)} %queries.1, bf16[2,8,24,640]{3,2,1,0:T(8,128)(2,1)} %bank.1, bf16[3,64,8,640]{3,2,1,0:T(8,128)(2,1)} %tokens.1, bf16[640,5120]{1,0:T(8,128)(2,1)} %weight.1), custom_call_target="tpu_custom_call" | custom-call | tf_op jit(solution)/shard_map/block/pallas_call | solution.py:292
  148.7 2.0 %copy.10 = bf16[8,8,5120]{2,1,0:T(8,128)(2,1)} copy(bf16[8,8,5120]{2,1,0:T(8,128)(2,1)} %bitcast.1) | data formatting | bytes 1310720

commit v2 on v1

v2 whole, which is shorter than its diff:
```python
import functools

import jax
import jax.numpy as jnp
from jax import lax
from jax.experimental import pallas as pl
from jax.experimental.pallas import tpu as pltpu
from jax.sharding import PartitionSpec as P

HEAD_DIM = 128
ROWS_Y = 4
CHUNKS = 4
EXP2_SCALE = HEAD_DIM ** -0.5 * 1.4426950408889634
FAR = 1e30
MESH = pl.DeviceIdType.MESH
scope = jax.named_scope


def dot_t(a, b):
    return lax.dot_general(a, b, (((1,), (1,)), ((), ())), preferred_element_type=jnp.float32)


def dot(a, b):
    return jnp.dot(a, b, preferred_element_type=jnp.float32)


def await_bytes(ref, sem):
    pltpu.make_async_copy(ref, ref, sem).wait()


def remote(src, dst, send, recv, **where):
    pltpu.make_async_remote_copy(
        src_ref=src, dst_ref=dst, send_sem=send, recv_sem=recv, device_id=where, device_id_type=MESH
    ).start()


def kernel(dims, slots, live, queries, bank, tokens, weight, out, *scratch):
    shards, levels, chips = dims
    held = (scratch[0:levels], scratch[levels:2 * levels])
    (picked, listed, qv, wv, qkv, o_here, o_back, ref_out, combined, part, pair, summed, half_l, half_r, full_l, full_r,
     local_sem, ring_send, ring_recv, pick_send, pick_recv, token_send, token_recv, o_send, o_recv, pair_send, pair_recv,
     half_send, half_recv, full_send, full_recv, own_sem) = scratch[2 * levels:]
    spatial, here, width = queries.shape
    heads = width // HEAD_DIM
    mine = spatial // shards
    half = levels // 2
    f = lax.axis_index("frames")
    r = lax.axis_index("heads")
    z, y = lax.div(f, ROWS_Y), lax.rem(f, ROWS_Y)
    x, core = lax.div(r, 2), lax.rem(r, 2)
    up = lax.rem(z + 1, levels) * ROWS_Y + y
    down = lax.rem(z + levels - 1, levels) * ROWS_Y + y
    twin = r + 1 - 2 * core
    right = lax.rem(x + 1, chips) * 2 + core
    left = lax.rem(x + chips - 1, chips) * 2 + core

    def peer(i):
        k, dy = lax.div(i, ROWS_Y), lax.rem(i, ROWS_Y)
        odd = lax.rem(k, 2)
        dz = odd * lax.div(k + 1, 2) + (1 - odd) * (levels - lax.div(k, 2))
        return lax.rem(z + dz, levels) * ROWS_Y + lax.rem(y + dy, ROWS_Y)

    own = [pltpu.make_async_copy(bank.at[kv], held[kv][0], local_sem.at[kv]) for kv in range(2)]
    load_q = pltpu.make_async_copy(queries, qv, local_sem.at[2])
    load_w = pltpu.make_async_copy(weight, wv, local_sem.at[3])
    keep = [pltpu.make_async_copy(tokens.at[:, mine * f + s], qkv.at[s, :, f], own_sem.at[0, s]) for s in range(mine)]
    for copy in (*own, load_q, *keep, load_w):
        copy.start()

    with scope("barrier"):
        barrier = pltpu.get_barrier_semaphore()

        @pl.loop(1, shards)
        def _(i):
            pl.semaphore_signal(barrier, inc=1, device_id={"frames": peer(i)}, device_id_type=MESH)

        for near in (twin, right, left):
            pl.semaphore_signal(barrier, inc=1, device_id={"heads": near}, device_id_type=MESH)
        pl.semaphore_wait(barrier, shards - 1 + 3)

    def pass_on(kv, src, rel, upward):
        ref = bank.at[kv] if src == 0 else held[kv][src]
        remote(ref, held[kv][rel], ring_send.at[kv, rel], ring_recv.at[kv, rel], frames=up if upward else down)

    def pick(kv, rel):
        for dy in range(ROWS_Y):
            shard = z * ROWS_Y + lax.rem(y + dy, ROWS_Y)
            for j in range(2):
                block = held[kv][rel][slots[j, shard]]
                if dy:
                    picked[kv, rel, dy - 1, j] = block
                else:
                    listed[kv, j, rel, 0] = block
        for dy in range(1, ROWS_Y):
            remote(
                picked.at[kv, rel, dy - 1], listed.at[kv, :, rel, dy], pick_send, pick_recv.at[kv],
                frames=z * ROWS_Y + lax.rem(y + dy, ROWS_Y),
            )

    def send_tokens(s, first, last):
        @pl.loop(first, last)
        def _(i):
            p = peer(i)
            remote(tokens.at[:, mine * p + s], qkv.at[s, :, f], token_send, token_recv.at[s], frames=p)

    def frame_attention(s):
        with scope(f"wait_tokens{s}"):
            keep[s].wait()
            await_bytes(qkv.at[s, :, pl.ds(1, shards - 1)], token_recv.at[s])

        def head(h, _):
            hs = pl.ds(pl.multiple_of(h * HEAD_DIM, HEAD_DIM), HEAD_DIM)
            q, k, v = (qkv[s, i, :, :, hs].reshape(shards * here, HEAD_DIM) for i in range(3))
            scores = dot_t(q, k)
            peak = jnp.max(scores, axis=1, keepdims=True)
            p = jnp.exp2((scores - peak) * EXP2_SCALE)
            got = dot(p.astype(jnp.bfloat16), v) / jnp.sum(p, axis=1, keepdims=True)
            o_here[s, :, :, hs] = got.astype(jnp.bfloat16).reshape(shards, here, HEAD_DIM)
            return 0

        with scope(f"frame_attention{s}"):
            lax.fori_loop(0, heads, head, 0)

        @pl.loop(1, shards)
        def _(i):
            p = peer(i)
            remote(o_here.at[s, p], o_back.at[s, f], o_send, o_recv.at[s], frames=p)

        pltpu.make_async_copy(o_here.at[s, f], o_back.at[s, f], own_sem.at[1, s]).start()

    alive = live[1, f] > 0
    keys = levels * ROWS_Y * listed.shape[4]

    def bank_head(h, _):
        hs = pl.ds(pl.multiple_of(h * HEAD_DIM, HEAD_DIM), HEAD_DIM)
        for block in range(2):
            rows = spatial // 2
            q = qv[pl.ds(block * rows, rows), :, hs].reshape(rows * here, HEAD_DIM)
            s0 = dot_t(q, listed[0, 0, :, :, :, hs].reshape(keys, HEAD_DIM))
            s1 = dot_t(q, listed[0, 1, :, :, :, hs].reshape(keys, HEAD_DIM))
            peak1 = jnp.max(s1, axis=1, keepdims=True)
            peak = jnp.max(s0, axis=1, keepdims=True)
            peak = jnp.where(alive, jnp.maximum(peak, peak1), peak)
            p0 = jnp.exp2((s0 - peak) * EXP2_SCALE)
            p1 = jnp.exp2((s1 - jnp.where(alive, peak, FAR)) * EXP2_SCALE)
            total = jnp.sum(p0, axis=1, keepdims=True) + jnp.sum(p1, axis=1, keepdims=True)
            got = dot(p0.astype(jnp.bfloat16), listed[1, 0, :, :, :, hs].reshape(keys, HEAD_DIM))
            got += dot(p1.astype(jnp.bfloat16), listed[1, 1, :, :, :, hs].reshape(keys, HEAD_DIM))
            ref_out[pl.ds(block * rows // mine, rows // mine), :, :, hs] = (got / total).reshape(
                rows // mine, mine, here, HEAD_DIM
            )
        return 0

    order = (lax.rem(x + 2, chips), lax.rem(x + 1, chips), lax.rem(x + chips - 1, chips), x)
    homes = shards // chips
    rows = homes * here // 2
    h2 = rows // 2
    chunk = weight.shape[1] // CHUNKS
    tile = chunk // 2

    def project(s):
        with scope(f"wait_o{s}"):
            pltpu.make_async_copy(o_here.at[s, f], o_back.at[s, f], own_sem.at[1, s]).wait()
            await_bytes(o_back.at[s, pl.ds(1, shards - 1)], o_recv.at[s])
        with scope(f"project{s}"):
            for k, dest in enumerate(order):
                at = pl.ds(pl.multiple_of(dest * homes, homes), homes)
                combined[pl.ds(k * 2 * rows, 2 * rows), :] = (
                    (ref_out[at, s] + o_back[s, at].astype(jnp.float32)).astype(jnp.bfloat16).reshape(2 * rows, width)
                )

            @pl.loop(0, CHUNKS)
            def _(n):
                for t in range(2):
                    cs = pl.ds(pl.multiple_of(n * chunk + t * tile, tile), tile)
                    part[s, n, :, :, :, pl.ds(t * tile, tile)] = (
                        dot(combined[...], wv[:, cs]).astype(jnp.bfloat16).reshape(chips, 2, rows, tile)
                    )
                remote(part.at[s, n, :, 1 - core], pair.at[s, n], pair_send, pair_recv.at[s, n], heads=twin)

    def both(s, n, k):
        return part[s, n, k, core].astype(jnp.float32) + pair[s, n, k].astype(jnp.float32)

    def first_hop(s):
        with scope(f"first_hop{s}"):
            @pl.loop(0, CHUNKS)
            def _(n):
                await_bytes(pair.at[s, n], pair_recv.at[s, n])
                summed[s, n, 0] = both(s, n, 0).astype(jnp.bfloat16)
                remote(summed.at[s, n, 0, pl.ds(0, h2)], half_l.at[s, n], half_send, half_recv.at[0, s, n], heads=right)
                remote(summed.at[s, n, 0, pl.ds(h2, h2)], half_r.at[s, n], half_send, half_recv.at[1, s, n], heads=left)

    def second_hop(s):
        with scope(f"second_hop{s}"):
            @pl.loop(0, CHUNKS)
            def _(n):
                await_bytes(half_l.at[s, n], half_recv.at[0, s, n])
                value = both(s, n, 1)
                top = value[:h2] + half_l[s, n].astype(jnp.float32)
                summed[s, n, 1, pl.ds(0, h2)] = top.astype(jnp.bfloat16)
                summed[s, n, 1, pl.ds(h2, h2)] = value[h2:].astype(jnp.bfloat16)
                remote(summed.at[s, n, 1], full_l.at[s, n], full_send, full_recv.at[0, s, n], heads=right)
                await_bytes(half_r.at[s, n], half_recv.at[1, s, n])
                value = both(s, n, 2)
                low = value[h2:] + half_r[s, n].astype(jnp.float32)
                summed[s, n, 2, pl.ds(0, h2)] = value[:h2].astype(jnp.bfloat16)
                summed[s, n, 2, pl.ds(h2, h2)] = low.astype(jnp.bfloat16)
                remote(summed.at[s, n, 2], full_r.at[s, n], full_send, full_recv.at[1, s, n], heads=left)

    def finish(s):
        with scope(f"finish{s}"):
            @pl.loop(0, CHUNKS)
            def _(n):
                await_bytes(full_l.at[s, n], full_recv.at[0, s, n])
                await_bytes(full_r.at[s, n], full_recv.at[1, s, n])
                value = both(s, n, 3) + full_l[s, n].astype(jnp.float32) + full_r[s, n].astype(jnp.float32)
                cs = pl.ds(pl.multiple_of(n * chunk, chunk), chunk)
                out[:, s, :, cs] = value.astype(jnp.bfloat16).reshape(homes // 2, here, chunk)

    with scope("own"):
        for kv in range(2):
            pass_on(kv, 0, 1, True)
            pass_on(kv, 0, levels - 1, False)
        for kv in range(2):
            own[kv].wait()
            pick(kv, 0)
    middle = shards // 2
    for step in range(1, half + 1):
        if step == half:
            send_tokens(0, 1, shards)
            send_tokens(1, 1, middle)
        with scope(f"ring{step}"):
            for kv in range(2):
                for rel, upward in ((step, True), (levels - step, False)):
                    if step == half and upward != (kv == 0):
                        continue
                    await_bytes(held[kv][rel], ring_recv.at[kv, rel])
                    last = half if upward == (kv == 0) else half - 1
                    if step < last:
                        pass_on(kv, rel, rel + 1 if upward else rel - 1, upward)
                    pick(kv, rel)

    frame_attention(0)
    send_tokens(1, middle, shards)
    with scope("wait_picks"):
        load_q.wait()
        for kv in range(2):
            await_bytes(listed.at[kv, :, :, pl.ds(1, ROWS_Y - 1)], pick_recv.at[kv])
    with scope("bank_attention"):
        lax.fori_loop(0, heads, bank_head, 0)
    load_w.wait()
    project(0)
    first_hop(0)
    frame_attention(1)
    second_hop(0)
    project(1)
    first_hop(1)
    finish(0)
    second_hop(1)
    finish(1)

    with scope("drain"):
        for kv in range(2):
            for rel in range(1, levels):
                await_bytes(held[kv][rel], ring_send.at[kv, rel])
        await_bytes(picked, pick_send)
        for s in range(mine):
            await_bytes(qkv.at[s, :, pl.ds(1, shards - 1)], token_send)
            await_bytes(o_back.at[s, pl.ds(1, shards - 1)], o_send)
        await_bytes(pair, pair_send)
        await_bytes(half_l, half_send)
        await_bytes(half_r, half_send)
        await_bytes(full_l, full_send)
        await_bytes(full_r, full_send)


def local(dims, bank_query, char_bank, char_slots, slot_live, frame_tokens, out_weight):
    shards, levels, chips = dims
    spatial, here, width = bank_query.shape
    _, characters, ref_here, _ = char_bank.shape
    mine = spatial // shards
    columns = out_weight.shape[1]
    homes = shards // chips
    rows = homes * here // 2
    chunk = columns // CHUNKS
    bf16, f32 = jnp.bfloat16, jnp.float32
    dma = pltpu.SemaphoreType.DMA
    vmem = pltpu.VMEM
    scratch = [vmem((characters, ref_here, width), bf16) for _ in range(2 * levels)] + [
        vmem((2, levels, ROWS_Y - 1, 2, ref_here, width), bf16),
        vmem((2, 2, levels, ROWS_Y, ref_here, width), bf16),
        vmem((spatial, here, width), bf16),
        vmem((width, columns), bf16),
        vmem((mine, 3, shards, here, width), bf16),
        vmem((mine, shards, here, width), bf16),
        vmem((mine, shards, here, width), bf16),
        vmem((shards, mine, here, width), f32),
        vmem((shards * here, width), bf16),
        vmem((mine, CHUNKS, chips, 2, rows, chunk), bf16),
        vmem((mine, CHUNKS, chips, rows, chunk), bf16),
        vmem((mine, CHUNKS, 3, rows, chunk), bf16),
        vmem((mine, CHUNKS, rows // 2, chunk), bf16),
        vmem((mine, CHUNKS, rows // 2, chunk), bf16),
        vmem((mine, CHUNKS, rows, chunk), bf16),
        vmem((mine, CHUNKS, rows, chunk), bf16),
        dma((4,)), dma((2, levels)), dma((2, levels)), dma(()), dma((2,)), dma(()), dma((mine,)), dma(()), dma((mine,)),
        dma(()), dma((mine, CHUNKS)), dma(()), dma((2, mine, CHUNKS)), dma(()), dma((2, mine, CHUNKS)), dma((2, mine)),
    ]
    smem = pl.BlockSpec(memory_space=pltpu.SMEM)
    anywhere = pl.BlockSpec(memory_space=pl.ANY)
    out = pl.pallas_call(
        functools.partial(kernel, dims),
        out_shape=jax.ShapeDtypeStruct((homes // 2, mine, here, columns), bf16),
        in_specs=[smem, smem, anywhere, anywhere, anywhere, anywhere],
        out_specs=pl.BlockSpec(memory_space=pltpu.VMEM),
        scratch_shapes=scratch,
        compiler_params=pltpu.CompilerParams(
            collective_id=0, has_side_effects=True, vmem_limit_bytes=60 * 1024 * 1024
        ),
        name="block",
    )(char_slots.T, slot_live.T, bank_query, char_bank, frame_tokens, out_weight)
    return out.reshape(homes // 2 * mine, here, columns)


def solution(mesh):
    shards = mesh.shape["frames"]
    dims = (shards, shards // ROWS_Y, mesh.shape["heads"] // 2)
    in_specs = (
        P(None, "frames", "heads"),
        P(None, None, "frames", "heads"),
        P(),
        P(),
        P(None, None, "frames", "heads"),
        P("heads", None),
    )
    return jax.shard_map(
        functools.partial(local, dims), mesh=mesh, in_specs=in_specs, out_specs=P("heads", "frames", None), check_vma=False
    )
```

time: 154 us -> 134 us (0.87); the launches traced: 151 us -> 133 us
  Pallas kernels: 146 us -> 131 us
  local copies, waits for them, and re-layouts: 4.69 us -> 1.97 us
    pallas_call x1, Pallas kernels: 146 us -> 131 us  [local(): pl.pallas_call(functools.partial(kernel, dims), out_shape=jax.ShapeDtypeS...]
    unnamed x3 -> x1, local copies, waits for them, and re-layouts: 4.69 us -> 1.97 us
where the time goes in v2:
time: 134 us; the launch traced here: 133 us
  Pallas kernels  131 us (98%)
  local copies, waits for them, and re-layouts  1.97 us (1%)
    pallas_call x1, Pallas kernels, local(): pl.pallas_call(functools.partial(kernel, dims), out_shape=jax.ShapeDtypeS...  131 us

profile of v2, /device:TPU:8, one launch (start us, length us, event | category | flops | bytes accessed | tf_op | source)
XLA Modules:
  0.0 132.8 jit_solution(568620016295622253)
XLA Ops:
  0.0 130.8 %block.1 = bf16[4,2,8,5120]{3,2,1,0:T(8,128)(2,1)} custom-call(s32[2,32]{1,0:T(2,128)} %bitcast.4, s32[2,32]{1,0:T(2,128)} %bitcast.5, bf16[64,8,640]{2,1,0:T(8,128)(2,1)} %queries.1, bf16[2,8,24,640]{3,2,1,0:T(8,128)(2,1)} %bank.1, bf16[3,64,8,640]{3,2,1,0:T(8,128)(2,1)} %tokens.1, bf16[640,5120]{1,0:T(8,128)(2,1)} %weight.1), custom_call_target="tpu_custom_call" | custom-call | tf_op jit(solution)/shard_map/block/pallas_call | solution.py:311
  130.8 2.0 %copy.8 = bf16[8,8,5120]{2,1,0:T(8,128)(2,1)} copy(bf16[8,8,5120]{2,1,0:T(8,128)(2,1)} %bitcast.3) | data formatting | bytes 1310720

commit v3 on v2

--- a/solution.py
+++ b/solution.py
@@ -10,6 +10,10 @@
 HEAD_DIM = 128
 ROWS_Y = 4
 CHUNKS = 4
+UNITS = 3
+EARLY = 4
+AHEAD = 6
+LAG = 2
 EXP2_SCALE = HEAD_DIM ** -0.5 * 1.4426950408889634
 FAR = 1e30
 MESH = pl.DeviceIdType.MESH
@@ -34,12 +38,18 @@
     ).start()
 
 
+def unit_rows(u, here):
+    return here * (ROWS_Y if u == 0 else ROWS_Y // 2)
+
+
 def kernel(dims, slots, live, queries, bank, tokens, weight, out, *scratch):
     shards, levels, chips = dims
     held = (scratch[0:levels], scratch[levels:2 * levels])
-    (picked, listed, qv, wv, qkv, o_here, o_back, ref_out, combined, part, pair, summed, half_l, half_r, full_l, full_r,
-     local_sem, ring_send, ring_recv, pick_send, pick_recv, token_send, token_recv, o_send, o_recv, pair_send, pair_recv,
-     half_send, half_recv, full_send, full_recv, own_sem) = scratch[2 * levels:]
+    (picked, listed, qv, wv, qkv, o_here, o_back, ref_out, combined) = scratch[2 * levels:2 * levels + 9]
+    buffers = scratch[2 * levels + 9:-16]
+    part, pair, summed, half_l, half_r, full_l, full_r = (buffers[i * UNITS:(i + 1) * UNITS] for i in range(7))
+    (local_sem, ring_send, ring_recv, pick_send, pick_recv, token_send, token_recv, o_send, o_recv, pair_send, pair_recv,
+     half_send, half_recv, full_send, full_recv, own_sem) = scratch[-16:]
     spatial, here, width = queries.shape
     heads = width // HEAD_DIM
     mine = spatial // shards
@@ -54,11 +64,21 @@
     right = lax.rem(x + 1, chips) * 2 + core
     left = lax.rem(x + chips - 1, chips) * 2 + core
 
-    def peer(i):
-        k, dy = lax.div(i, ROWS_Y), lax.rem(i, ROWS_Y)
+    colour = lax.rem(z + y, 2)
+
+    def place(k, dy):
         odd = lax.rem(k, 2)
         dz = odd * lax.div(k + 1, 2) + (1 - odd) * (levels - lax.div(k, 2))
-        return lax.rem(z + dz, levels) * ROWS_Y + lax.rem(y + dy, ROWS_Y)
+        return lax.rem(z + dz, levels), lax.rem(y + dy, ROWS_Y)
+
+    def peer(i):
+        there_z, there_y = place(lax.div(i, ROWS_Y), lax.rem(i, ROWS_Y))
+        return there_z * ROWS_Y + there_y
+
+    def peer_of(i, wanted):
+        there_z, _ = place(lax.div(i, 2), 0)
+        dy = lax.rem(there_z + y + wanted, 2) + 2 * lax.rem(i, 2)
+        return there_z * ROWS_Y + lax.rem(y + dy, ROWS_Y)
 
     own = [pltpu.make_async_copy(bank.at[kv], held[kv][0], local_sem.at[kv]) for kv in range(2)]
     load_q = pltpu.make_async_copy(queries, qv, local_sem.at[2])
@@ -103,7 +123,15 @@
             p = peer(i)
             remote(tokens.at[:, mine * p + s], qkv.at[s, :, f], token_send, token_recv.at[s], frames=p)
 
+    def send_coloured(s, wanted, first, last):
+        @pl.loop(first if first else lax.rem(colour + wanted + 1, 2), last)
+        def _(i):
+            p = peer_of(i, wanted)
+            remote(tokens.at[:, mine * p + s], qkv.at[s, :, f], token_send, token_recv.at[s], frames=p)
+
     def frame_attention(s):
+        unit = s * (1 + colour)
+
         with scope(f"wait_tokens{s}"):
             keep[s].wait()
             await_bytes(qkv.at[s, :, pl.ds(1, shards - 1)], token_recv.at[s])
@@ -124,9 +152,9 @@
         @pl.loop(1, shards)
         def _(i):
             p = peer(i)
-            remote(o_here.at[s, p], o_back.at[s, f], o_send, o_recv.at[s], frames=p)
-
-        pltpu.make_async_copy(o_here.at[s, f], o_back.at[s, f], own_sem.at[1, s]).start()
+            remote(o_here.at[s, p], o_back.at[s, f], o_send, o_recv.at[unit], frames=p)
+
+        pltpu.make_async_copy(o_here.at[s, f], o_back.at[s, f], o_recv.at[unit]).start()
 
     alive = live[1, f] > 0
     keys = levels * ROWS_Y * listed.shape[4]
@@ -153,82 +181,95 @@
 
     order = (lax.rem(x + 2, chips), lax.rem(x + 1, chips), lax.rem(x + chips - 1, chips), x)
     homes = shards // chips
-    rows = homes * here // 2
-    h2 = rows // 2
     chunk = weight.shape[1] // CHUNKS
     tile = chunk // 2
 
-    def project(s):
-        with scope(f"wait_o{s}"):
-            pltpu.make_async_copy(o_here.at[s, f], o_back.at[s, f], own_sem.at[1, s]).wait()
-            await_bytes(o_back.at[s, pl.ds(1, shards - 1)], o_recv.at[s])
-        with scope(f"project{s}"):
+    def project(u):
+        s = min(u, 1)
+        rows = unit_rows(u, here)
+        with scope(f"wait_o{u}"):
+            await_bytes(o_back.at[s, pl.ds(0, shards if u == 0 else shards // 2)], o_recv.at[u])
+        with scope(f"project{u}"):
             for k, dest in enumerate(order):
-                at = pl.ds(pl.multiple_of(dest * homes, homes), homes)
-                combined[pl.ds(k * 2 * rows, 2 * rows), :] = (
-                    (ref_out[at, s] + o_back[s, at].astype(jnp.float32)).astype(jnp.bfloat16).reshape(2 * rows, width)
-                )
-
+                for c in range(2):
+                    base = pl.multiple_of(dest * homes, homes) + c * ROWS_Y
+                    at = (k * 2 + c) * rows
+                    if u == 0:
+                        span = pl.ds(base, ROWS_Y)
+                        value = ref_out[span, s] + o_back[s, span].astype(jnp.float32)
+                        combined[pl.ds(at, rows), :] = value.astype(jnp.bfloat16).reshape(rows, width)
+                        continue
+                    for j in range(2):
+                        p = base + (u - 1 + c) % 2 + 2 * j
+                        value = ref_out[p, s] + o_back[s, p].astype(jnp.float32)
+                        combined[pl.ds(at + j * here, here), :] = value.astype(jnp.bfloat16)
+            for n in range(CHUNKS + LAG):
+                if n < CHUNKS:
+                    for t in range(2):
+                        cs = pl.ds(n * chunk + t * tile, tile)
+                        part[u][n, :, :, :, pl.ds(t * tile, tile)] = (
+                            dot(combined[pl.ds(0, chips * 2 * rows), :], wv[:, cs])
+                            .astype(jnp.bfloat16).reshape(chips, 2, rows, tile)
+                        )
+                    remote(part[u].at[n, :, 1 - core], pair[u].at[n], pair_send, pair_recv.at[u, n], heads=twin)
+                if n >= LAG and u:
+                    first_hop(u, n - LAG)
+
+    def both(u, n, k):
+        return part[u][n, k, core].astype(jnp.float32) + pair[u][n, k].astype(jnp.float32)
+
+    def first_hop(u, n):
+        h2 = unit_rows(u, here) // 2
+        await_bytes(pair[u].at[n], pair_recv.at[u, n])
+        summed[u][n, 0] = both(u, n, 0).astype(jnp.bfloat16)
+        remote(summed[u].at[n, 0, pl.ds(0, h2)], half_l[u].at[n], half_send, half_recv.at[0, u, n], heads=right)
+        remote(summed[u].at[n, 0, pl.ds(h2, h2)], half_r[u].at[n], half_send, half_recv.at[1, u, n], heads=left)
+
+    def second_hop(u):
+        h2 = unit_rows(u, here) // 2
+        with scope(f"second_hop{u}"):
             @pl.loop(0, CHUNKS)
             def _(n):
-                for t in range(2):
-                    cs = pl.ds(pl.multiple_of(n * chunk + t * tile, tile), tile)
-                    part[s, n, :, :, :, pl.ds(t * tile, tile)] = (
-                        dot(combined[...], wv[:, cs]).astype(jnp.bfloat16).reshape(chips, 2, rows, tile)
-                    )
-                remote(part.at[s, n, :, 1 - core], pair.at[s, n], pair_send, pair_recv.at[s, n], heads=twin)
-
-    def both(s, n, k):
-        return part[s, n, k, core].astype(jnp.float32) + pair[s, n, k].astype(jnp.float32)
-
-    def first_hop(s):
-        with scope(f"first_hop{s}"):
+                await_bytes(half_l[u].at[n], half_recv.at[0, u, n])
+                value = both(u, n, 1)
+                top = value[:h2] + half_l[u][n].astype(jnp.float32)
+                summed[u][n, 1, pl.ds(0, h2)] = top.astype(jnp.bfloat16)
+                summed[u][n, 1, pl.ds(h2, h2)] = value[h2:].astype(jnp.bfloat16)
+                remote(summed[u].at[n, 1], full_l[u].at[n], full_send, full_recv.at[0, u, n], heads=right)
+                await_bytes(half_r[u].at[n], half_recv.at[1, u, n])
+                value = both(u, n, 2)
+                low = value[h2:] + half_r[u][n].astype(jnp.float32)
+                summed[u][n, 2, pl.ds(0, h2)] = value[:h2].astype(jnp.bfloat16)
+                summed[u][n, 2, pl.ds(h2, h2)] = low.astype(jnp.bfloat16)
+                remote(summed[u].at[n, 2], full_r[u].at[n], full_send, full_recv.at[1, u, n], heads=left)
+
+    def finish(u):
+        with scope(f"finish{u}"):
             @pl.loop(0, CHUNKS)
             def _(n):
-                await_bytes(pair.at[s, n], pair_recv.at[s, n])
-                summed[s, n, 0] = both(s, n, 0).astype(jnp.bfloat16)
-                remote(summed.at[s, n, 0, pl.ds(0, h2)], half_l.at[s, n], half_send, half_recv.at[0, s, n], heads=right)
-                remote(summed.at[s, n, 0, pl.ds(h2, h2)], half_r.at[s, n], half_send, half_recv.at[1, s, n], heads=left)
-
-    def second_hop(s):
-        with scope(f"second_hop{s}"):
-            @pl.loop(0, CHUNKS)
-            def _(n):
-                await_bytes(half_l.at[s, n], half_recv.at[0, s, n])
-                value = both(s, n, 1)
-                top = value[:h2] + half_l[s, n].astype(jnp.float32)
-                summed[s, n, 1, pl.ds(0, h2)] = top.astype(jnp.bfloat16)
-                summed[s, n, 1, pl.ds(h2, h2)] = value[h2:].astype(jnp.bfloat16)
-                remote(summed.at[s, n, 1], full_l.at[s, n], full_send, full_recv.at[0, s, n], heads=right)
-                await_bytes(half_r.at[s, n], half_recv.at[1, s, n])
-                value = both(s, n, 2)
-                low = value[h2:] + half_r[s, n].astype(jnp.float32)
-                summed[s, n, 2, pl.ds(0, h2)] = value[:h2].astype(jnp.bfloat16)
-                summed[s, n, 2, pl.ds(h2, h2)] = low.astype(jnp.bfloat16)
-                remote(summed.at[s, n, 2], full_r.at[s, n], full_send, full_recv.at[1, s, n], heads=left)
-
-    def finish(s):
-        with scope(f"finish{s}"):
-            @pl.loop(0, CHUNKS)
-            def _(n):
-                await_bytes(full_l.at[s, n], full_recv.at[0, s, n])
-                await_bytes(full_r.at[s, n], full_recv.at[1, s, n])
-                value = both(s, n, 3) + full_l[s, n].astype(jnp.float32) + full_r[s, n].astype(jnp.float32)
+                await_bytes(full_l[u].at[n], full_recv.at[0, u, n])
+                await_bytes(full_r[u].at[n], full_recv.at[1, u, n])
+                value = both(u, n, 3) + full_l[u][n].astype(jnp.float32) + full_r[u][n].astype(jnp.float32)
+                value = value.astype(jnp.bfloat16)
                 cs = pl.ds(pl.multiple_of(n * chunk, chunk), chunk)
-                out[:, s, :, cs] = value.astype(jnp.bfloat16).reshape(homes // 2, here, chunk)
+                if u == 0:
+                    out[:, 0, :, cs] = value.reshape(ROWS_Y, here, chunk)
+                else:
+                    for j in range(2):
+                        out[lax.rem(u - 1 + core, 2) + 2 * j, 1, :, cs] = value[j * here:(j + 1) * here]
 
     with scope("own"):
         for kv in range(2):
             pass_on(kv, 0, 1, True)
             pass_on(kv, 0, levels - 1, False)
+        send_tokens(0, 1, EARLY)
         for kv in range(2):
             own[kv].wait()
             pick(kv, 0)
-    middle = shards // 2
     for step in range(1, half + 1):
         if step == half:
-            send_tokens(0, 1, shards)
-            send_tokens(1, 1, middle)
+            send_tokens(0, EARLY, shards)
+            send_coloured(1, 0, 0, AHEAD)
         with scope(f"ring{step}"):
             for kv in range(2):
                 for rel, upward in ((step, True), (levels - step, False)):
@@ -241,7 +282,8 @@
                     pick(kv, rel)
 
     frame_attention(0)
-    send_tokens(1, middle, shards)
+    send_coloured(1, 0, AHEAD, shards // 2)
+    send_coloured(1, 1, 0, shards // 2)
     with scope("wait_picks"):
         load_q.wait()
         for kv in range(2):
@@ -250,14 +292,28 @@
         lax.fori_loop(0, heads, bank_head, 0)
     load_w.wait()
     project(0)
-    first_hop(0)
-    frame_attention(1)
+
+    with scope("first_hop0"):
+        for n in range(CHUNKS):
+            first_hop(0, n)
+
+    @pl.when(colour == 0)
+    def _():
+        frame_attention(1)
+
     second_hop(0)
+
+    @pl.when(colour == 1)
+    def _():
+        frame_attention(1)
+
     project(1)
-    first_hop(1)
     finish(0)
     second_hop(1)
+    project(2)
     finish(1)
+    second_hop(2)
+    finish(2)
 
     with scope("drain"):
         for kv in range(2):
@@ -267,11 +323,12 @@
         for s in range(mine):
             await_bytes(qkv.at[s, :, pl.ds(1, shards - 1)], token_send)
             await_bytes(o_back.at[s, pl.ds(1, shards - 1)], o_send)
-        await_bytes(pair, pair_send)
-        await_bytes(half_l, half_send)
-        await_bytes(half_r, half_send)
-        await_bytes(full_l, full_send)
-        await_bytes(full_r, full_send)
+        for u in range(UNITS):
+            await_bytes(pair[u], pair_send)
+            await_bytes(half_l[u], half_send)
+            await_bytes(half_r[u], half_send)
+            await_bytes(full_l[u], full_send)
+            await_bytes(full_r[u], full_send)
 
 
 def local(dims, bank_query, char_bank, char_slots, slot_live, frame_tokens, out_weight):
@@ -281,8 +338,8 @@
     mine = spatial // shards
     columns = out_weight.shape[1]
     homes = shards // chips
-    rows = homes * here // 2
     chunk = columns // CHUNKS
+    rows = [unit_rows(u, here) for u in range(UNITS)]
     bf16, f32 = jnp.bfloat16, jnp.float32
     dma = pltpu.SemaphoreType.DMA
     vmem = pltpu.VMEM
@@ -296,15 +353,13 @@
         vmem((mine, shards, here, width), bf16),
         vmem((shards, mine, here, width), f32),
         vmem((shards * here, width), bf16),
-        vmem((mine, CHUNKS, chips, 2, rows, chunk), bf16),
-        vmem((mine, CHUNKS, chips, rows, chunk), bf16),
-        vmem((mine, CHUNKS, 3, rows, chunk), bf16),
-        vmem((mine, CHUNKS, rows // 2, chunk), bf16),
-        vmem((mine, CHUNKS, rows // 2, chunk), bf16),
-        vmem((mine, CHUNKS, rows, chunk), bf16),
-        vmem((mine, CHUNKS, rows, chunk), bf16),
-        dma((4,)), dma((2, levels)), dma((2, levels)), dma(()), dma((2,)), dma(()), dma((mine,)), dma(()), dma((mine,)),
-        dma(()), dma((mine, CHUNKS)), dma(()), dma((2, mine, CHUNKS)), dma(()), dma((2, mine, CHUNKS)), dma((2, mine)),
+        *[vmem((CHUNKS, chips, 2, n, chunk), bf16) for n in rows],
+        *[vmem((CHUNKS, chips, n, chunk), bf16) for n in rows],
+        *[vmem((CHUNKS, 3, n, chunk), bf16) for n in rows],
+        *[vmem((CHUNKS, n // 2, chunk), bf16) for n in rows * 2],
+        *[vmem((CHUNKS, n, chunk), bf16) for n in rows * 2],
+        dma((4,)), dma((2, levels)), dma((2, levels)), dma(()), dma((2,)), dma(()), dma((mine,)), dma(()), dma((UNITS,)),
+        dma(()), dma((UNITS, CHUNKS)), dma(()), dma((2, UNITS, CHUNKS)), dma(()), dma((2, UNITS, CHUNKS)), dma((1, mine)),
     ]
     smem = pl.BlockSpec(memory_space=pltpu.SMEM)
     anywhere = pl.BlockSpec(memory_space=pl.ANY)

time: 134 us -> 130 us (0.970)
  Pallas kernels: 131 us -> 126 us
    pallas_call x1, Pallas kernels: 131 us -> 126 us  [local(): pl.pallas_call(functools.partial(kernel, dims), out_shape=jax.ShapeDtypeS...]
where the time goes in v3:
time: 130 us; the launch traced here: 128 us
  Pallas kernels  126 us (97%)
  local copies, waits for them, and re-layouts  1.97 us (2%)
    pallas_call x1, Pallas kernels, local(): pl.pallas_call(functools.partial(kernel, dims), out_shape=jax.ShapeDtypeS...  126 us

profile of v3, /device:TPU:8, one launch (start us, length us, event | category | flops | bytes accessed | tf_op | source)
XLA Modules:
  0.0 128.3 jit_solution(2516710005504169668)
XLA Ops:
  0.0 126.3 %block.1 = bf16[4,2,8,5120]{3,2,1,0:T(8,128)(2,1)} custom-call(s32[2,32]{1,0:T(2,128)} %bitcast.4, s32[2,32]{1,0:T(2,128)} %bitcast.5, bf16[64,8,640]{2,1,0:T(8,128)(2,1)} %queries.1, bf16[2,8,24,640]{3,2,1,0:T(8,128)(2,1)} %bank.1, bf16[3,64,8,640]{3,2,1,0:T(8,128)(2,1)} %tokens.1, bf16[640,5120]{1,0:T(8,128)(2,1)} %weight.1), custom_call_target="tpu_custom_call" | custom-call | tf_op jit(solution)/shard_map/block/pallas_call | solution.py:366
  126.3 2.0 %copy.8 = bf16[8,8,5120]{2,1,0:T(8,128)(2,1)} copy(bf16[8,8,5120]{2,1,0:T(8,128)(2,1)} %bitcast.3) | data formatting | bytes 1310720

commit v4 on v3

--- a/solution.py
+++ b/solution.py
@@ -14,6 +14,7 @@
 EARLY = 4
 AHEAD = 6
 LAG = 2
+START = 2
 EXP2_SCALE = HEAD_DIM ** -0.5 * 1.4426950408889634
 FAR = 1e30
 MESH = pl.DeviceIdType.MESH
@@ -42,14 +43,14 @@
     return here * (ROWS_Y if u == 0 else ROWS_Y // 2)
 
 
-def kernel(dims, slots, live, queries, bank, tokens, weight, out, *scratch):
+def kernel(dims, slots, live, queries, bank, tokens, weight, out_hbm, *scratch):
     shards, levels, chips = dims
     held = (scratch[0:levels], scratch[levels:2 * levels])
-    (picked, listed, qv, wv, qkv, o_here, o_back, ref_out, combined) = scratch[2 * levels:2 * levels + 9]
-    buffers = scratch[2 * levels + 9:-16]
+    (picked, listed, qv, wv, qkv, o_here, o_back, ref_out, combined, out) = scratch[2 * levels:2 * levels + 10]
+    buffers = scratch[2 * levels + 10:-17]
     part, pair, summed, half_l, half_r, full_l, full_r = (buffers[i * UNITS:(i + 1) * UNITS] for i in range(7))
     (local_sem, ring_send, ring_recv, pick_send, pick_recv, token_send, token_recv, o_send, o_recv, pair_send, pair_recv,
-     half_send, half_recv, full_send, full_recv, own_sem) = scratch[-16:]
+     half_send, half_recv, full_send, full_recv, own_sem, out_sem) = scratch[-17:]
     spatial, here, width = queries.shape
     heads = width // HEAD_DIM
     mine = spatial // shards
@@ -72,6 +73,7 @@
         return lax.rem(z + dz, levels), lax.rem(y + dy, ROWS_Y)
 
     def peer(i):
+        i = shards - i
         there_z, there_y = place(lax.div(i, ROWS_Y), lax.rem(i, ROWS_Y))
         return there_z * ROWS_Y + there_y
 
@@ -124,9 +126,11 @@
             remote(tokens.at[:, mine * p + s], qkv.at[s, :, f], token_send, token_recv.at[s], frames=p)
 
     def send_coloured(s, wanted, first, last):
-        @pl.loop(first if first else lax.rem(colour + wanted + 1, 2), last)
+        end = last if last < shards // 2 else last - lax.rem(colour + wanted + 1, 2)
+
+        @pl.loop(first, end)
         def _(i):
-            p = peer_of(i, wanted)
+            p = peer_of(shards // 2 - 1 - i, wanted)
             remote(tokens.at[:, mine * p + s], qkv.at[s, :, f], token_send, token_recv.at[s], frames=p)
 
     def frame_attention(s):
@@ -184,7 +188,7 @@
     chunk = weight.shape[1] // CHUNKS
     tile = chunk // 2
 
-    def project(u):
+    def project(u, between=None):
         s = min(u, 1)
         rows = unit_rows(u, here)
         with scope(f"wait_o{u}"):
@@ -212,6 +216,8 @@
                             .astype(jnp.bfloat16).reshape(chips, 2, rows, tile)
                         )
                     remote(part[u].at[n, :, 1 - core], pair[u].at[n], pair_send, pair_recv.at[u, n], heads=twin)
+                if between is not None and n < CHUNKS:
+                    between(n)
                 if n >= LAG and u:
                     first_hop(u, n - LAG)
 
@@ -226,22 +232,25 @@
         remote(summed[u].at[n, 0, pl.ds(h2, h2)], half_r[u].at[n], half_send, half_recv.at[1, u, n], heads=left)
 
     def second_hop(u):
-        h2 = unit_rows(u, here) // 2
         with scope(f"second_hop{u}"):
             @pl.loop(0, CHUNKS)
             def _(n):
-                await_bytes(half_l[u].at[n], half_recv.at[0, u, n])
-                value = both(u, n, 1)
-                top = value[:h2] + half_l[u][n].astype(jnp.float32)
-                summed[u][n, 1, pl.ds(0, h2)] = top.astype(jnp.bfloat16)
-                summed[u][n, 1, pl.ds(h2, h2)] = value[h2:].astype(jnp.bfloat16)
-                remote(summed[u].at[n, 1], full_l[u].at[n], full_send, full_recv.at[0, u, n], heads=right)
-                await_bytes(half_r[u].at[n], half_recv.at[1, u, n])
-                value = both(u, n, 2)
-                low = value[h2:] + half_r[u][n].astype(jnp.float32)
-                summed[u][n, 2, pl.ds(0, h2)] = value[:h2].astype(jnp.bfloat16)
-                summed[u][n, 2, pl.ds(h2, h2)] = low.astype(jnp.bfloat16)
-                remote(summed[u].at[n, 2], full_r[u].at[n], full_send, full_recv.at[1, u, n], heads=left)
+                second_hop_chunk(u, n)
+
+    def second_hop_chunk(u, n):
+        h2 = unit_rows(u, here) // 2
+        await_bytes(half_l[u].at[n], half_recv.at[0, u, n])
+        value = both(u, n, 1)
+        top = value[:h2] + half_l[u][n].astype(jnp.float32)
+        summed[u][n, 1, pl.ds(0, h2)] = top.astype(jnp.bfloat16)
+        summed[u][n, 1, pl.ds(h2, h2)] = value[h2:].astype(jnp.bfloat16)
+        remote(summed[u].at[n, 1], full_l[u].at[n], full_send, full_recv.at[0, u, n], heads=right)
+        await_bytes(half_r[u].at[n], half_recv.at[1, u, n])
+        value = both(u, n, 2)
+        low = value[h2:] + half_r[u][n].astype(jnp.float32)
+        summed[u][n, 2, pl.ds(0, h2)] = value[:h2].astype(jnp.bfloat16)
+        summed[u][n, 2, pl.ds(h2, h2)] = low.astype(jnp.bfloat16)
+        remote(summed[u].at[n, 2], full_r[u].at[n], full_send, full_recv.at[1, u, n], heads=left)
 
     def finish(u):
         with scope(f"finish{u}"):
@@ -254,21 +263,24 @@
                 cs = pl.ds(pl.multiple_of(n * chunk, chunk), chunk)
                 if u == 0:
                     out[:, 0, :, cs] = value.reshape(ROWS_Y, here, chunk)
+                    pltpu.make_async_copy(out.at[:, 0, :, cs], out_hbm.at[:, 0, :, cs], out_sem).start()
                 else:
                     for j in range(2):
-                        out[lax.rem(u - 1 + core, 2) + 2 * j, 1, :, cs] = value[j * here:(j + 1) * here]
+                        at = lax.rem(u - 1 + core, 2) + 2 * j
+                        out[at, 1, :, cs] = value[j * here:(j + 1) * here]
+                        pltpu.make_async_copy(out.at[at, 1, :, cs], out_hbm.at[at, 1, :, cs], out_sem).start()
 
     with scope("own"):
         for kv in range(2):
             pass_on(kv, 0, 1, True)
             pass_on(kv, 0, levels - 1, False)
-        send_tokens(0, 1, EARLY)
+        send_tokens(0, shards - EARLY + 1, shards)
         for kv in range(2):
             own[kv].wait()
             pick(kv, 0)
     for step in range(1, half + 1):
         if step == half:
-            send_tokens(0, EARLY, shards)
+            send_tokens(0, 1, shards - EARLY + 1)
             send_coloured(1, 0, 0, AHEAD)
         with scope(f"ring{step}"):
             for kv in range(2):
@@ -284,6 +296,7 @@
     frame_attention(0)
     send_coloured(1, 0, AHEAD, shards // 2)
     send_coloured(1, 1, 0, shards // 2)
+
     with scope("wait_picks"):
         load_q.wait()
         for kv in range(2):
@@ -309,13 +322,15 @@
 
     project(1)
     finish(0)
-    second_hop(1)
-    project(2)
+    for n in range(START):
+        second_hop_chunk(1, n)
+    project(2, lambda n: second_hop_chunk(1, n + START) if n + START < CHUNKS else None)
+    second_hop(2)
     finish(1)
-    second_hop(2)
     finish(2)
 
     with scope("drain"):
+        await_bytes(out, out_sem)
         for kv in range(2):
             for rel in range(1, levels):
                 await_bytes(held[kv][rel], ring_send.at[kv, rel])
@@ -353,13 +368,14 @@
         vmem((mine, shards, here, width), bf16),
         vmem((shards, mine, here, width), f32),
         vmem((shards * here, width), bf16),
+        vmem((homes // 2, mine, here, columns), bf16),
         *[vmem((CHUNKS, chips, 2, n, chunk), bf16) for n in rows],
         *[vmem((CHUNKS, chips, n, chunk), bf16) for n in rows],
         *[vmem((CHUNKS, 3, n, chunk), bf16) for n in rows],
         *[vmem((CHUNKS, n // 2, chunk), bf16) for n in rows * 2],
         *[vmem((CHUNKS, n, chunk), bf16) for n in rows * 2],
         dma((4,)), dma((2, levels)), dma((2, levels)), dma(()), dma((2,)), dma(()), dma((mine,)), dma(()), dma((UNITS,)),
-        dma(()), dma((UNITS, CHUNKS)), dma(()), dma((2, UNITS, CHUNKS)), dma(()), dma((2, UNITS, CHUNKS)), dma((1, mine)),
+        dma(()), dma((UNITS, CHUNKS)), dma(()), dma((2, UNITS, CHUNKS)), dma(()), dma((2, UNITS, CHUNKS)), dma((1, mine)), dma(()),
     ]
     smem = pl.BlockSpec(memory_space=pltpu.SMEM)
     anywhere = pl.BlockSpec(memory_space=pl.ANY)
@@ -367,7 +383,7 @@
         functools.partial(kernel, dims),
         out_shape=jax.ShapeDtypeStruct((homes // 2, mine, here, columns), bf16),
         in_specs=[smem, smem, anywhere, anywhere, anywhere, anywhere],
-        out_specs=pl.BlockSpec(memory_space=pltpu.VMEM),
+        out_specs=anywhere,
         scratch_shapes=scratch,
         compiler_params=pltpu.CompilerParams(
             collective_id=0, has_side_effects=True, vmem_limit_bytes=60 * 1024 * 1024

time: 130 us -> 128 us (0.985)
    pallas_call x1, Pallas kernels: 126 us -> 125 us  [local(): pl.pallas_call(functools.partial(kernel, dims), out_shape=jax.ShapeDtypeS...]
where the time goes in v4:
time: 128 us; the launch traced here: 127 us
  Pallas kernels  125 us (98%)
  local copies, waits for them, and re-layouts  1.97 us (2%)
    pallas_call x1, Pallas kernels, local(): pl.pallas_call(functools.partial(kernel, dims), out_shape=jax.ShapeDtypeS...  125 us

profile of v4, /device:TPU:8, one launch (start us, length us, event | category | flops | bytes accessed | tf_op | source)
XLA Modules:
  0.0 126.6 jit_solution(15434323754866325499)
XLA Ops:
  0.0 124.6 %block.1 = bf16[4,2,8,5120]{3,2,1,0:T(8,128)(2,1)} custom-call(s32[2,32]{1,0:T(2,128)} %bitcast.4, s32[2,32]{1,0:T(2,128)} %bitcast.5, bf16[64,8,640]{2,1,0:T(8,128)(2,1)} %queries.1, bf16[2,8,24,640]{3,2,1,0:T(8,128)(2,1)} %bank.1, bf16[3,64,8,640]{3,2,1,0:T(8,128)(2,1)} %tokens.1, bf16[640,5120]{1,0:T(8,128)(2,1)} %weight.1), custom_call_target="tpu_custom_call" | custom-call | tf_op jit(solution)/shard_map/block/pallas_call | solution.py:382
  124.7 2.0 %copy.8 = bf16[8,8,5120]{2,1,0:T(8,128)(2,1)} copy(bf16[8,8,5120]{2,1,0:T(8,128)(2,1)} %bitcast.3) | data formatting | bytes 1310720

commit v5 on v4

--- a/solution.py
+++ b/solution.py
@@ -14,7 +14,6 @@
 EARLY = 4
 AHEAD = 6
 LAG = 2
-START = 2
 EXP2_SCALE = HEAD_DIM ** -0.5 * 1.4426950408889634
 FAR = 1e30
 MESH = pl.DeviceIdType.MESH
@@ -151,7 +150,7 @@
             return 0
 
         with scope(f"frame_attention{s}"):
-            lax.fori_loop(0, heads, head, 0)
+            lax.fori_loop(0, heads, head, 0, unroll=True)
 
         @pl.loop(1, shards)
         def _(i):
@@ -294,8 +293,12 @@
                     pick(kv, rel)
 
     frame_attention(0)
-    send_coloured(1, 0, AHEAD, shards // 2)
-    send_coloured(1, 1, 0, shards // 2)
+
+    def send_rest():
+        send_coloured(1, 0, AHEAD, shards // 2)
+        send_coloured(1, 1, 0, shards // 2)
+
+    pl.when(core == 1)(send_rest)
 
     with scope("wait_picks"):
         load_q.wait()
@@ -303,6 +306,7 @@
             await_bytes(listed.at[kv, :, :, pl.ds(1, ROWS_Y - 1)], pick_recv.at[kv])
     with scope("bank_attention"):
         lax.fori_loop(0, heads, bank_head, 0)
+    pl.when(core == 0)(send_rest)
     load_w.wait()
     project(0)
 
@@ -322,9 +326,12 @@
 
     project(1)
     finish(0)
-    for n in range(START):
-        second_hop_chunk(1, n)
-    project(2, lambda n: second_hop_chunk(1, n + START) if n + START < CHUNKS else None)
+
+    def second_hops(n):
+        for m in ((), (0, 1), (2,), (3,))[n]:
+            second_hop_chunk(1, m)
+
+    project(2, second_hops)
     second_hop(2)
     finish(1)
     finish(2)

time: 128 us -> 127 us (level)
  no operation moved by 1% of the time
where the time goes in v5:
time: 127 us
  Pallas kernels  125 us (98%)
  local copies, waits for them, and re-layouts  1.97 us (2%)
    pallas_call x1, Pallas kernels, local(): pl.pallas_call(functools.partial(kernel, dims), out_shape=jax.ShapeDtypeS...  125 us

profile of v5, /device:TPU:8, one launch (start us, length us, event | category | flops | bytes accessed | tf_op | source)
XLA Modules:
  0.0 126.7 jit_solution(6225469820147666466)
XLA Ops:
  0.0 124.7 %block.1 = bf16[4,2,8,5120]{3,2,1,0:T(8,128)(2,1)} custom-call(s32[2,32]{1,0:T(2,128)} %bitcast.4, s32[2,32]{1,0:T(2,128)} %bitcast.5, bf16[64,8,640]{2,1,0:T(8,128)(2,1)} %queries.1, bf16[2,8,24,640]{3,2,1,0:T(8,128)(2,1)} %bank.1, bf16[3,64,8,640]{3,2,1,0:T(8,128)(2,1)} %tokens.1, bf16[640,5120]{1,0:T(8,128)(2,1)} %weight.1), custom_call_target="tpu_custom_call" | custom-call | tf_op jit(solution)/shard_map/block/pallas_call | solution.py:389
  124.7 2.0 %copy.8 = bf16[8,8,5120]{2,1,0:T(8,128)(2,1)} copy(bf16[8,8,5120]{2,1,0:T(8,128)(2,1)} %bitcast.3) | data formatting | bytes 1310720
